TPU v7x, 32 devices: a whole 2x2x4 slice. The times are simulated.
32 devices in a mesh: gz: 2 (over y), row: 4 (over x, core), col: 4 (over z).
Axes of the slice: x: 2, y: 2, z: 4, core: 2. Of those that a mesh axis runs over, the one named last changes fastest.
Arguments:
- anc_lower: bfloat16 [1, 1024, 1024], P(None, 'col', 'row'), may hold values from -0.125 to 0.125
- anc_upper: bfloat16 [1, 1024, 1024], P(None, 'col', 'row'), may hold values from -0.125 to 0.125
- sub_lower: bfloat16 [16, 1024, 1024], P('gz', 'col', 'row'), may hold values from -0.125 to 0.125
- sub_upper: bfloat16 [16, 1024, 1024], P('gz', 'col', 'row'), may hold values from -0.125 to 0.125
- anc_rhs: bfloat16 [1, 1024, 64], P(None, 'col'), may hold values from -6 to 6
- sub_rhs: bfloat16 [6, 1024, 64], P('gz', 'col'), may hold values from -6 to 6
- layer_subtree: int32 [2], replicated, may hold values from 0 to 1, each once
- sub_pattern: int32 [10, 2], P('gz'), may hold values 0 or 1
Outputs:
- anc_solution: float32 [1, 1024, 64], P(None, ('row', 'col'))
- sub_solution: float32 [6, 1024, 64], P('gz', ('row', 'col'))
Inputs may be any that keep to these rules, and one draw needn't show every extreme that they name: `layer_subtree`: each subtree is held by exactly one layer.
All inputs are finite; a program needn't handle non-finite values. No bound on the sum of `sub_pattern` on one device may be relied on, other than what follows from the above.
Results may differ from a plain program's by a relative error of at most 0.018.
Values may be sent and summed in bfloat16 or wider, within the bound.
A program may use at most 64 MiB of HBM per device.

v0:
```python
import jax
import jax.numpy as jnp
import numpy as np
from jax import lax
from jax.sharding import PartitionSpec as P

R = 64
SUB_LEVELS = 2
SUB_NODES = 3


def level_span(depth_now):
    return (2**depth_now - 1, 2 ** (depth_now + 1) - 1)


def local_routes(first_id, stop_id, depth_now, target_count):
    table = np.zeros((target_count, (stop_id - first_id) * depth_now), np.float32)
    for offset, member in enumerate(range(first_id, stop_id)):
        for local_level in range(depth_now):
            target = (member + 1 >> depth_now - local_level) - 1
            table[target, offset * depth_now + local_level] = 1.0
    return table


def solve_diagonal(residual, blocks):
    whole_blocks = lax.all_gather(blocks, "col", axis=1, tiled=True)
    whole_res = lax.all_gather(residual, "col", axis=1, tiled=True)
    rows_full = jnp.einsum(
        "nki,nkr->nir", whole_blocks, whole_res, preferred_element_type=jnp.float32
    )
    share = rows_full.shape[1] // lax.axis_size("col")
    owned = lax.dynamic_slice_in_dim(rows_full, lax.axis_index("col") * share, share, 1)
    return (owned, rows_full.astype(jnp.bfloat16))


def upper_sum(values):
    return lax.psum(values, "row")


def local(anc_lower, anc_upper, sub_lower, sub_upper, anc_rhs, sub_rhs, layer_subtree, sub_pattern):
    layers = lax.axis_size("gz")
    levels = layers.bit_length() - 1
    anc_count = layers - 1
    row_count = lax.axis_size("row")
    col_count = lax.axis_size("col")
    rows_here = anc_lower.shape[2]
    cols_here = anc_lower.shape[1]
    sub_start = [0]
    for member in range(SUB_NODES):
        sub_start.append(sub_start[-1] + levels + (member + 1).bit_length() - 1)
    anc_start = [0]
    for member in range(anc_count):
        anc_start.append(anc_start[-1] + (member + 1).bit_length() - 1)
    low_pattern = sub_pattern[:, 0].astype(jnp.float32)
    up_pattern = sub_pattern[:, 1].astype(jnp.float32)
    layer_here = lax.axis_index("gz")
    subtree = jnp.sum(
        jnp.where(jnp.arange(layers, dtype=jnp.int32) == layer_here, layer_subtree, 0)
    )
    powers = jnp.asarray(2 ** (levels - np.arange(levels)), jnp.int32)
    heap_ids = (subtree + layers) // powers - 1
    choose = (heap_ids[:, None] == jnp.arange(anc_count, dtype=jnp.int32)[None, :]).astype(
        jnp.float32
    )
    first_layer = (layer_here == 0).astype(jnp.float32)
    row_index = lax.axis_index("row")
    col_index = lax.axis_index("col")
    holds_piece = (row_index == col_index * row_count // col_count).astype(jnp.float32)
    piece_start = jnp.clip(col_index * cols_here - row_index * rows_here, 0, rows_here - cols_here)

    def own_piece(rows_block):
        return holds_piece * lax.dynamic_slice_in_dim(rows_block, piece_start, cols_here, 1).astype(
            jnp.float32
        )

    sub_acc = jnp.zeros((SUB_NODES, cols_here, R), jnp.float32)
    to_anc = jnp.zeros((anc_count, cols_here, R), jnp.float32)
    sub_rows = {}
    for depth_now in reversed(range(SUB_LEVELS)):
        first_id, stop_id = level_span(depth_now)
        node_count = stop_id - first_id
        given = sub_rhs[first_id:stop_id].astype(jnp.float32)
        if depth_now + 1 < SUB_LEVELS:
            given = given - lax.psum(sub_acc[first_id:stop_id], "row")
        unused, solved = solve_diagonal(given.astype(jnp.bfloat16), sub_lower[first_id:stop_id])
        sub_rows[depth_now] = solved
        per_node = levels + depth_now
        opening = SUB_NODES + sub_start[first_id]
        blocks = sub_lower[opening : opening + node_count * per_node].reshape(
            node_count, per_node, cols_here, rows_here
        )
        weights = low_pattern[sub_start[first_id] : sub_start[stop_id]].reshape(
            node_count, per_node
        )
        updates = jnp.einsum("npik,nkr->npir", blocks, solved, preferred_element_type=jnp.float32)
        updates = updates * weights[:, :, None, None]
        to_anc = to_anc + jnp.einsum("ea,eir->air", choose, jnp.sum(updates[:, :levels], 0))
        if depth_now > 0:
            table = jnp.asarray(local_routes(first_id, stop_id, depth_now, SUB_NODES))
            sub_acc = sub_acc + jnp.einsum(
                "tq,qir->tir", table, updates[:, levels:].reshape(-1, cols_here, R)
            )
    anc_acc = jnp.zeros((anc_count, cols_here, R), jnp.float32)
    anc_rows = {}
    for depth_now in reversed(range(levels)):
        first_id, stop_id = level_span(depth_now)
        node_count = stop_id - first_id
        joined = to_anc[first_id:stop_id] + first_layer * anc_acc[first_id:stop_id]
        reached = lax.psum(joined, ("gz", "row"))
        given = anc_rhs[first_id:stop_id].astype(jnp.float32) - reached
        unused, solved = solve_diagonal(given.astype(jnp.bfloat16), anc_lower[first_id:stop_id])
        anc_rows[depth_now] = solved
        if depth_now > 0:
            opening = anc_count + anc_start[first_id]
            blocks = anc_lower[opening : opening + node_count * depth_now].reshape(
                node_count, depth_now, cols_here, rows_here
            )
            updates = jnp.einsum(
                "npik,nkr->npir", blocks, solved, preferred_element_type=jnp.float32
            )
            table = jnp.asarray(local_routes(first_id, stop_id, depth_now, anc_count))
            anc_acc = anc_acc + jnp.einsum("tq,qir->tir", table, updates.reshape(-1, cols_here, R))
    anc_z_parts = []
    anc_out_parts = []
    for depth_now in range(levels):
        first_id, stop_id = level_span(depth_now)
        node_count = stop_id - first_id
        given = own_piece(anc_rows[depth_now])
        if depth_now > 0:
            z_sofar = jnp.concatenate(anc_z_parts, 0)
            table = local_routes(first_id, stop_id, depth_now, anc_count)[:first_id].T
            sources = jnp.einsum(
                "qa,akr->qkr",
                jnp.asarray(table, jnp.bfloat16),
                z_sofar,
                preferred_element_type=jnp.float32,
            )
            sources = sources.astype(jnp.bfloat16).reshape(node_count, depth_now, rows_here, R)
            opening = anc_count + anc_start[first_id]
            blocks = anc_upper[opening : opening + node_count * depth_now].reshape(
                node_count, depth_now, cols_here, rows_here
            )
            updates = jnp.einsum(
                "npik,npkr->npir", blocks, sources, preferred_element_type=jnp.float32
            )
            given = given - jnp.sum(updates, 1)
        summed = upper_sum(given)
        owned, solved = solve_diagonal(summed.astype(jnp.bfloat16), anc_upper[first_id:stop_id])
        anc_out_parts.append(owned)
        anc_z_parts.append(solved)
    anc_z_all = jnp.concatenate(anc_z_parts, 0)
    selected = jnp.einsum(
        "ea,akr->ekr", choose.astype(jnp.bfloat16), anc_z_all, preferred_element_type=jnp.float32
    )
    selected = selected.astype(jnp.bfloat16)
    sub_z_parts = []
    sub_out_parts = []
    for depth_now in range(SUB_LEVELS):
        first_id, stop_id = level_span(depth_now)
        node_count = stop_id - first_id
        per_node = levels + depth_now
        opening = SUB_NODES + sub_start[first_id]
        blocks = sub_upper[opening : opening + node_count * per_node].reshape(
            node_count, per_node, cols_here, rows_here
        )
        weights = up_pattern[sub_start[first_id] : sub_start[stop_id]].reshape(node_count, per_node)
        updates = jnp.einsum(
            "npik,pkr->npir", blocks[:, :levels], selected, preferred_element_type=jnp.float32
        )
        if depth_now > 0:
            z_sofar = sub_z_parts[0]
            table = local_routes(first_id, stop_id, depth_now, SUB_NODES)[:first_id].T
            sources = jnp.einsum(
                "qa,akr->qkr",
                jnp.asarray(table, jnp.bfloat16),
                z_sofar,
                preferred_element_type=jnp.float32,
            )
            sources = sources.astype(jnp.bfloat16).reshape(node_count, depth_now, rows_here, R)
            local_updates = jnp.einsum(
                "npik,npkr->npir", blocks[:, levels:], sources, preferred_element_type=jnp.float32
            )
            updates = jnp.concatenate([updates, local_updates], 1)
        change = jnp.sum(updates * weights[:, :, None, None], 1)
        summed = upper_sum(own_piece(sub_rows[depth_now]) - change)
        owned, solved = solve_diagonal(summed.astype(jnp.bfloat16), sub_upper[first_id:stop_id])
        sub_out_parts.append(owned)
        sub_z_parts.append(solved)
    return (jnp.concatenate(anc_out_parts, 0), jnp.concatenate(sub_out_parts, 0))


def solution(mesh):
    in_specs = (
        P(None, "col", "row"),
        P(None, "col", "row"),
        P("gz", "col", "row"),
        P("gz", "col", "row"),
        P(None, "col", None),
        P("gz", "col", None),
        P(),
        P("gz", None),
    )
    out_specs = (P(None, ("row", "col"), None), P("gz", ("row", "col"), None))
    return jax.shard_map(local, mesh=mesh, in_specs=in_specs, out_specs=out_specs, check_vma=False)
```

profile of v0, /device:TPU:0, one launch (start us, length us, event | category | flops | bytes accessed | tf_op | source)
XLA Modules:
  0.0 251.9 jit_solution(8480645708661849595)
XLA Ops:
  7.2 1.7 slice.67
  9.0 0.6 copy-done.7
  9.6 0.6 fusion.35
  11.0 0.7 copy-done.6
  11.8 17.3 %all_gather.37 = bf16[2,1024,64]{1,2,0:T(8,128)(2,1)S(1)} all-gather(bf16[2,256,64]{1,2,0:T(8,128)(2,1)S(1)} %slice-done.3), channel_id=1, replica_groups=mesh['gz'=2,'row'=4,'col'=4] {'col'}, dimensions={1}, use_global_device_ids=true | all-gather | bytes 327680 | tf_op jit(solution)/shard_map/all_gather | solution.py:27
  29.1 22.6 %all_gather.39 = bf16[1,1024,256]{2,1,0:T(8,128)(2,1)S(1)} all-gather(bf16[1,256,256]{2,1,0:T(8,128)(2,1)S(1)} %slice-done.1), channel_id=1, replica_groups=mesh['gz'=2,'row'=4,'col'=4] {'col'}, dimensions={1}, use_global_device_ids=true | all-gather | bytes 655360 | tf_op jit(solution)/shard_map/all_gather | solution.py:26
  51.7 1.6 convolution_convert_fusion
  53.4 0.3 fusion
  53.7 0.3 copy-done.8
  54.0 0.9 fusion.27
  55.0 30.0 %all-reduce.4.cloned.1.call-done = f32[1,256,64]{1,0,2:T(1,128)} async-done(((f32[1,256,64]{1,0,2:T(1,128)}), f32[1,256,64]{1,0,2:T(1,128)}) %all-reduce.4.cloned.1.call-update) | async-done | bytes 65552 | tf_op jit(solution)/shard_map/psum | solution.py:84
  85.0 0.9 fusion.30
  85.9 13.5 %all_gather.38 = bf16[1,1024,64]{1,0,2:T(2,128)(2,1)S(1)} all-gather(bf16[1,256,64]{1,0,2:T(2,128)(2,1)S(1)} %fusion.30), channel_id=1, replica_groups=mesh['gz'=2,'row'=4,'col'=4] {'col'}, dimensions={1}, use_global_device_ids=true | all-gather | bytes 163840 | tf_op jit(solution)/shard_map/all_gather | solution.py:27
  99.4 0.2 convolution_convert_fusion.2
  99.6 0.9 fusion.7
  100.5 0.7 slice.87
  101.4 0.8 copy-done.3
  102.2 14.9 %all_gather.41 = bf16[1,1024,256]{2,1,0:T(8,128)(2,1)S(1)} all-gather(bf16[1,256,256]{2,1,0:T(8,128)(2,1)S(1)} %copy-done.3), channel_id=1, replica_groups=mesh['gz'=2,'row'=4,'col'=4] {'col'}, dimensions={1}, use_global_device_ids=true | all-gather | bytes 655360 | tf_op jit(solution)/shard_map/all_gather | solution.py:26
  117.1 16.3 %all_gather.43 = bf16[1,1024,256]{2,1,0:T(8,128)(2,1)S(1)} all-gather(bf16[1,256,256]{2,1,0:T(8,128)(2,1)S(1)} %copy-done.4), channel_id=1, replica_groups=mesh['gz'=2,'row'=4,'col'=4] {'col'}, dimensions={1}, use_global_device_ids=true | all-gather | bytes 655360 | tf_op jit(solution)/shard_map/all_gather | solution.py:26
  133.4 14.8 %all_gather.45 = bf16[1,1024,256]{2,1,0:T(8,128)(2,1)S(1)} all-gather(bf16[1,256,256]{2,1,0:T(8,128)(2,1)S(1)} %slice-done.2), channel_id=1, replica_groups=mesh['gz'=2,'row'=4,'col'=4] {'col'}, dimensions={1}, use_global_device_ids=true | all-gather | bytes 655360 | tf_op jit(solution)/shard_map/all_gather | solution.py:26
  148.5 2.8 %all-reduce.6.cloned.1.call-done = f32[1,256,64]{1,2,0:T(8,128)} async-done(((f32[1,256,64]{1,2,0:T(8,128)}), f32[1,256,64]{1,2,0:T(8,128)}) %all-reduce.6.cloned.1.call-update) | async-done | bytes 65552 | tf_op jit(solution)/shard_map/psum | solution.py:109
  151.3 0.8 subtract_convert_fusion
  152.1 13.9 %all_gather.40 = bf16[1,1024,64]{1,2,0:T(8,128)(2,1)S(1)} all-gather(bf16[1,256,64]{1,2,0:T(8,128)(2,1)S(1)} %subtract_convert_fusion), channel_id=1, replica_groups=mesh['gz'=2,'row'=4,'col'=4] {'col'}, dimensions={1}, use_global_device_ids=true | all-gather | bytes 163840 | tf_op jit(solution)/shard_map/all_gather | solution.py:27
  166.2 11.5 %psum.37 = bf16[1,256,64]{1,2,0:T(8,128)(2,1)S(1)} all-reduce(f32[1,256,64]{1,2,0:T(8,128)S(1)} %fusion.10), channel_id=1, replica_groups=mesh['gz'=2,'row'=4,'col'=4] {'row'}, use_global_device_ids=true, to_apply=%region_4.5 | all-reduce | flops 16384 | bytes 98304 | tf_op jit(solution)/shard_map/psum | solution.py:37
  177.7 13.4 %all_gather.42 = bf16[1,1024,64]{1,2,0:T(8,128)(2,1)S(1)} all-gather(bf16[1,256,64]{1,2,0:T(8,128)(2,1)S(1)} %psum.37), channel_id=1, replica_groups=mesh['gz'=2,'row'=4,'col'=4] {'col'}, dimensions={1}, use_global_device_ids=true | all-gather | bytes 163840 | tf_op jit(solution)/shard_map/all_gather | solution.py:27
  191.5 10.7 %psum.38 = bf16[1,256,64]{1,2,0:T(8,128)(2,1)S(1)} all-reduce(f32[1,256,64]{1,2,0:T(8,128)S(1)} %fusion.3), channel_id=1, replica_groups=mesh['gz'=2,'row'=4,'col'=4] {'row'}, use_global_device_ids=true, to_apply=%region_5.6 | all-reduce | flops 16384 | bytes 98304 | tf_op jit(solution)/shard_map/psum | solution.py:37
  202.2 13.3 %all_gather.44 = bf16[1,1024,64]{1,2,0:T(8,128)(2,1)S(1)} all-gather(bf16[1,256,64]{1,2,0:T(8,128)(2,1)S(1)} %psum.38), channel_id=1, replica_groups=mesh['gz'=2,'row'=4,'col'=4] {'col'}, dimensions={1}, use_global_device_ids=true | all-gather | bytes 163840 | tf_op jit(solution)/shard_map/all_gather | solution.py:27
  216.3 11.9 %all-reduce.7 = bf16[2,256,64]{1,2,0:T(8,128)(2,1)S(1)} all-reduce(f32[2,256,64]{1,2,0:T(8,128)S(1)} %multiply_subtract_fusion), channel_id=1, replica_groups=mesh['gz'=2,'row'=4,'col'=4] {'row'}, use_global_device_ids=true, to_apply=%region_7.8 | all-reduce | flops 32768 | bytes 196608 | tf_op jit(solution)/shard_map/psum | solution.py:37
  228.2 14.0 %all_gather.46 = bf16[2,1024,64]{1,2,0:T(8,128)(2,1)S(1)} all-gather(bf16[2,256,64]{1,2,0:T(8,128)(2,1)S(1)} %all-reduce.7), channel_id=1, replica_groups=mesh['gz'=2,'row'=4,'col'=4] {'col'}, dimensions={1}, use_global_device_ids=true | all-gather | bytes 327680 | tf_op jit(solution)/shard_map/all_gather | solution.py:27
  242.3 1.5 fusion.36
  243.9 0.7 copy.24
  244.7 0.7 copy.23
  (56 shorter events, 2.4 us)
Async XLA Ops:
  7.2 44.6 %all-gather.3.cloned.1.call-start = ((), (), s32[]{:S(2)}) async-start(), calls=%async_computation | async-start | bytes 1310720 | tf_op jit(solution)/shard_map/all_gather | solution.py:26
  8.9 76.1 %all-reduce.4.cloned.1.call-start = ((), (), s32[]{:S(2)}) async-start(), calls=%async_computation.1 | async-start | bytes 131072 | tf_op jit(solution)/shard_map/psum | solution.py:84
  9.0 0.7 copy-start.7
  10.9 0.9 slice-start.3
  10.9 0.7 copy-start.6
  11.8 17.3 %slice-start.1 = ((bf16[8,256,256]{2,1,0:T(8,128)(2,1)}), bf16[1,256,256]{2,1,0:T(8,128)(2,1)S(1)}, s32[]{:S(2)}) async-start(bf16[8,256,256]{2,1,0:T(8,128)(2,1)} %param.13), calls=%async_computation.5 | async-start | bytes 262144 | tf_op jit(solution)/shard_map/slice | solution.py:85
  51.7 1.6 slice-start
  53.3 0.7 copy-start.8
  53.3 31.7 %slice-start.4 = ((bf16[3,256,64]{1,2,0:T(8,128)(2,1)}), bf16[1,256,64]{1,2,0:T(8,128)(2,1)S(1)}, s32[]{:S(2)}) async-start(bf16[3,256,64]{1,2,0:T(8,128)(2,1)} %param.16), calls=%async_computation.8 | async-start | bytes 65536 | tf_op jit(solution)/shard_map/slice | solution.py:82
  53.6 46.0 %copy-start = (bf16[8,256,256]{2,1,0:T(8,128)(2,1)S(1)}, bf16[8,256,256]{2,1,0:T(8,128)(2,1)}, u32[]{:S(2)}) copy-start(bf16[8,256,256]{2,1,0:T(8,128)(2,1)} %param.13) | copy-start | bytes 3145732
  54.0 46.5 %copy-start.1 = (bf16[8,256,256]{2,1,0:T(8,128)(2,1)S(1)}, bf16[8,256,256]{2,1,0:T(8,128)(2,1)}, u32[]{:S(2)}) copy-start(bf16[8,256,256]{2,1,0:T(8,128)(2,1)} %param.14) | copy-start | bytes 3145732
  54.9 96.3 %all-reduce.6.cloned.1.call-start = ((), (), s32[]{:S(2)}) async-start(), calls=%async_computation.2 | async-start | bytes 131072 | tf_op jit(solution)/shard_map/psum | solution.py:109
  100.5 141.8 %all-gather.5.cloned.1.call-start = ((), (), s32[]{:S(2)}) async-start(), calls=%async_computation.3 | async-start | bytes 1310720 | tf_op jit(solution)/shard_map/all_gather | solution.py:26
  101.3 0.9 copy-start.3
  102.2 14.9 %copy-start.4 = (bf16[1,256,256]{2,1,0:T(8,128)(2,1)S(1)}, bf16[1,256,256]{2,1,0:T(8,128)(2,1)}, u32[]{:S(2)}) copy-start(bf16[1,256,256]{2,1,0:T(8,128)(2,1)} %param.12) | copy-start | bytes 393220
  117.1 16.3 %slice-start.2 = ((bf16[8,256,256]{2,1,0:T(8,128)(2,1)}), bf16[1,256,256]{2,1,0:T(8,128)(2,1)S(1)}, s32[]{:S(2)}) async-start(bf16[8,256,256]{2,1,0:T(8,128)(2,1)} %param.14), calls=%async_computation.6 | async-start | bytes 262144 | tf_op jit(solution)/shard_map/slice | solution.py:186
  133.4 17.9 %copy-start.5 = (bf16[1,256,64]{1,2,0:T(8,128)(2,1)S(1)}, bf16[1,256,64]{1,2,0:T(8,128)(2,1)}, u32[]{:S(2)}) copy-start(bf16[1,256,64]{1,2,0:T(8,128)(2,1)} %param.15) | copy-start | bytes 98308
  148.2 43.1 %copy-start.2 = (bf16[8,256,256]{2,1,0:T(8,128)(2,1)S(1)}, bf16[8,256,256]{2,1,0:T(8,128)(2,1)}, u32[]{:S(2)}) copy-start(bf16[8,256,256]{2,1,0:T(8,128)(2,1)} %param.14) | copy-start | bytes 3145732
Sparse Core Ops, SparseCore 0:
  9.5 40.4 all-gather.2
  55.0 29.9 all-reduce.3
  100.6 50.5 all-reduce.5
  152.7 27.7 all-gather.4
where the time goes:
time: 253 us; the launch traced here: 252 us
  blocking collectives  188 us (74%)
  waiting for transfers between devices  32.9 us (13%)
  between operations  14.7 us (6%)
  local copies, waits for them, and re-layouts  7.11 us (3%)
  matrix products  6.59 us (3%)
    all_gather x6, blocking collectives, solve_diagonal(): whole_res = lax.all_gather(residual, 'col', axis=1, tiled=True)  85.3 us
    all_gather x4, blocking collectives, solve_diagonal(): whole_blocks = lax.all_gather(blocks, 'col', axis=1, tiled=True)  68.6 us
    psum x3, blocking collectives, upper_sum(): return lax.psum(values, 'row')  34 us
    psum x1, waiting for transfers between devices, local(): given = given - lax.psum(sub_acc[first_id:stop_id], 'row')  30 us
  transfers between devices with their start and end apart: 4, of which 2 were waited for; matrix products, arithmetic and copies ran while one was open for 2% of the time, Pallas kernels for 0%

commit v1 on v0

--- a/solution.py
+++ b/solution.py
@@ -23,11 +23,39 @@
 
 
 def solve_diagonal(residual, blocks):
-    whole_blocks = lax.all_gather(blocks, "col", axis=1, tiled=True)
     whole_res = lax.all_gather(residual, "col", axis=1, tiled=True)
-    rows_full = jnp.einsum(
-        "nki,nkr->nir", whole_blocks, whole_res, preferred_element_type=jnp.float32
-    )
+    length, index, width = (lax.axis_size("col"), lax.axis_index("col"), blocks.shape[1])
+    right = [(i, (i + 1) % length) for i in range(length)]
+    backward = [(i, (i - 1) % length) for i in range(length)]
+    middle = length // 2
+    from_left = from_right = blocks
+    total = jnp.einsum(
+        "nki,nkr->nir",
+        blocks,
+        lax.dynamic_slice_in_dim(whole_res, index * width, blocks.shape[1], axis=1),
+        preferred_element_type=jnp.float32,
+    )
+    for step in range(1, middle + 1):
+        from_left = lax.ppermute(from_left, "col", right)
+        if step < length - middle:
+            from_right = lax.ppermute(from_right, "col", backward)
+            total = total + jnp.einsum(
+                "nki,nkr->nir",
+                from_right,
+                lax.dynamic_slice_in_dim(
+                    whole_res, (index + step) % length * width, from_right.shape[1], axis=1
+                ),
+                preferred_element_type=jnp.float32,
+            )
+        total = total + jnp.einsum(
+            "nki,nkr->nir",
+            from_left,
+            lax.dynamic_slice_in_dim(
+                whole_res, (index - step) % length * width, from_left.shape[1], axis=1
+            ),
+            preferred_element_type=jnp.float32,
+        )
+    rows_full = total
     share = rows_full.shape[1] // lax.axis_size("col")
     owned = lax.dynamic_slice_in_dim(rows_full, lax.axis_index("col") * share, share, 1)
     return (owned, rows_full.astype(jnp.bfloat16))

time: 253 us -> 294 us (1.16)
  waiting for transfers between devices: 32.9 us -> 111 us
  blocking collectives: 188 us -> 121 us
  starting transfers between devices: 0.16 us -> 22.7 us
  matrix products: 6.59 us -> 14.5 us
    all_gather x4 -> x0, blocking collectives: 68.6 us -> none  [solve_diagonal(): whole_blocks = lax.all_gather(blocks, 'col', axis=1, tiled=True)]
    psum x1, waiting for transfers between devices: 2.79 us -> 51.9 us  [local(): reached = lax.psum(joined, ('gz', 'row'))]
    ppermute x0 -> x18, waiting for transfers between devices: none -> 29.1 us  [the longest x12 29.1 us: solve_diagonal(): from_left = lax.ppermute(from_left, 'col', right)]
    ppermute x0 -> x18, starting transfers between devices: none -> 22.6 us  [the longest x6 17.1 us: solve_diagonal(): from_right = lax.ppermute(from_right, 'col', backward)]
    dot_general x6 -> x24, matrix products: 3.94 us -> 11.8 us  [the longest x12 5.52 us: solve_diagonal(): jnp.einsum('nki,nkr->nir', from_left, lax.dynamic_slice_in_dim(whole_res,...]
  transfers between devices with their start and end apart: 4 -> 20, of which waited for: 2 -> 6; matrix products, arithmetic and copies ran while one was open for 2% -> 7% of each run, Pallas kernels for 0% -> 0%
where the time goes in v1:
time: 294 us; the launch traced here: 293 us
  blocking collectives  121 us (41%)
  waiting for transfers between devices  111 us (38%)
  starting transfers between devices  22.7 us (8%)
  between operations  15 us (5%)
  matrix products  14.5 us (5%)
  local copies, waits for them, and re-layouts  5.82 us (2%)
    all_gather x6, blocking collectives, solve_diagonal(): whole_res = lax.all_gather(residual, 'col', axis=1, tiled=True)  88.1 us
    psum x1, waiting for transfers between devices, local(): reached = lax.psum(joined, ('gz', 'row'))  51.9 us
    psum x3, blocking collectives, upper_sum(): return lax.psum(values, 'row')  33.1 us
    psum x1, waiting for transfers between devices, local(): given = given - lax.psum(sub_acc[first_id:stop_id], 'row')  30 us
    ppermute x12, waiting for transfers between devices, solve_diagonal(): from_left = lax.ppermute(from_left, 'col', right)  29.1 us
    ppermute x6, starting transfers between devices, solve_diagonal(): from_right = lax.ppermute(from_right, 'col', backward)  17.1 us
  transfers between devices with their start and end apart: 20, of which 6 were waited for; matrix products, arithmetic and copies ran while one was open for 7% of the time, Pallas kernels for 0%

profile of v1, /device:TPU:0, one launch (start us, length us, event | category | flops | bytes accessed | tf_op | source)
XLA Modules:
  0.0 293.0 jit_solution(10155903407123012346)
XLA Ops:
  8.3 5.1 %collective-permute-start = (bf16[2,256,256]{2,1,0:T(8,128)(2,1)S(1)}, bf16[2,256,256]{2,1,0:T(8,128)(2,1)S(1)}, u32[]{:S(2)}, u32[]{:S(2)}) collective-permute-start(bf16[2,256,256]{2,1,0:T(8,128)(2,1)S(1)} %slice.68), channel_id=1, source_target_pairs={{0,3},{1,0},{2,1},{3,2},{4,7},{5,4},{6,5},{7,6},{8,11},{9,8},{10,9... | collective-permute-start | bytes 786440 | tf_op jit(solution)/shard_map/ppermute | solution.py:41
  13.4 1.6 slice.76
  15.0 3.8 %collective-permute-start.3 = (bf16[1,256,256]{2,1,0:T(8,128)(2,1)}, bf16[1,256,256]{2,1,0:T(8,128)(2,1)}, u32[]{:S(2)}, u32[]{:S(2)}) collective-permute-start(bf16[1,256,256]{2,1,0:T(8,128)(2,1)} %slice.76), channel_id=1, source_target_pairs={{0,3},{1,0},{2,1},{3,2},{4,7},{5,4},{6,5},{7,6},{8,11},{9,8},{10,9... | collective-permute-start | bytes 393224 | tf_op jit(solution)/shard_map/ppermute | solution.py:41
  18.8 3.8 %collective-permute-start.6 = (bf16[1,256,256]{2,1,0:T(8,128)(2,1)}, bf16[1,256,256]{2,1,0:T(8,128)(2,1)}, u32[]{:S(2)}, u32[]{:S(2)}) collective-permute-start(bf16[1,256,256]{2,1,0:T(8,128)(2,1)} %param.11), channel_id=1, source_target_pairs={{0,3},{1,0},{2,1},{3,2},{4,7},{5,4},{6,5},{7,6},{8,11},{9,8},{10,9... | collective-permute-start | bytes 393224 | tf_op jit(solution)/shard_map/ppermute | solution.py:41
  23.3 19.2 %all_gather.18 = bf16[2,1024,64]{1,2,0:T(8,128)(2,1)S(1)} all-gather(bf16[2,256,64]{1,2,0:T(8,128)(2,1)S(1)} %slice-done.1), channel_id=1, replica_groups=mesh['gz'=2,'row'=4,'col'=4] {'col'}, dimensions={1}, use_global_device_ids=true | all-gather | bytes 327680 | tf_op jit(solution)/shard_map/all_gather | solution.py:26
  44.1 2.2 collective-permute-start.7
  46.8 8.3 %collective-permute-done.2 = bf16[2,256,256]{2,1,0:T(8,128)(2,1)S(1)} collective-permute-done((bf16[2,256,256]{2,1,0:T(8,128)(2,1)S(1)}, bf16[2,256,256]{2,1,0:T(8,128)(2,1)S(1)}, u32[]{:S(2)}, u32[]{:S(2)}) %collective-permute-start.2) | collective-permute-done | bytes 262176 | tf_op jit(solution)/shard_map/ppermute | solution.py:39
  55.1 1.3 collective-permute-start.9
  58.0 30.0 %all-reduce.4.cloned.1.call-done = f32[1,256,64]{1,0,2:T(1,128)} async-done(((f32[1,256,64]{1,0,2:T(1,128)}), f32[1,256,64]{1,0,2:T(1,128)}) %all-reduce.4.cloned.1.call-update) | async-done | bytes 65552 | tf_op jit(solution)/shard_map/psum | solution.py:112
  88.9 13.5 %all_gather.19 = bf16[1,1024,64]{1,0,2:T(2,128)(2,1)S(1)} all-gather(bf16[1,256,64]{1,0,2:T(2,128)(2,1)S(1)} %fusion.43), channel_id=1, replica_groups=mesh['gz'=2,'row'=4,'col'=4] {'col'}, dimensions={1}, use_global_device_ids=true | all-gather | bytes 163840 | tf_op jit(solution)/shard_map/all_gather | solution.py:26
  102.9 1.0 convolution_add_fusion.14
  104.0 1.1 convolution_add_fusion.13
  105.0 7.7 %collective-permute-done.5 = bf16[1,256,256]{2,1,0:T(8,128)(2,1)S(1)} collective-permute-done((bf16[1,256,256]{2,1,0:T(8,128)(2,1)}, bf16[1,256,256]{2,1,0:T(8,128)(2,1)S(1)}, u32[]{:S(2)}, u32[]{:S(2)}) %collective-permute-start.5) | collective-permute-done | bytes 131104 | tf_op jit(solution)/shard_map/ppermute | solution.py:39
  114.1 51.9 %all-reduce.6.cloned.1.call-done = f32[1,256,64]{1,2,0:T(8,128)} async-done(((f32[1,256,64]{1,2,0:T(8,128)}), f32[1,256,64]{1,2,0:T(8,128)}) %all-reduce.6.cloned.1.call-update) | async-done | bytes 65552 | tf_op jit(solution)/shard_map/psum | solution.py:137
  166.9 13.4 %all_gather.20 = bf16[1,1024,64]{1,2,0:T(8,128)(2,1)S(1)} all-gather(bf16[1,256,64]{1,2,0:T(8,128)(2,1)S(1)} %subtract_convert_fusion), channel_id=1, replica_groups=mesh['gz'=2,'row'=4,'col'=4] {'col'}, dimensions={1}, use_global_device_ids=true | all-gather | bytes 163840 | tf_op jit(solution)/shard_map/all_gather | solution.py:26
  180.3 1.0 fusion.29
  181.3 1.5 collective-permute-start.13
  183.0 1.0 convolution_add_fusion.11
  184.0 1.1 convolution_add_fusion.10
  185.1 5.6 %collective-permute-done.8 = bf16[1,256,256]{2,1,0:T(8,128)(2,1)S(1)} collective-permute-done((bf16[1,256,256]{2,1,0:T(8,128)(2,1)}, bf16[1,256,256]{2,1,0:T(8,128)(2,1)S(1)}, u32[]{:S(2)}, u32[]{:S(2)}) %collective-permute-start.8) | collective-permute-done | bytes 131104 | tf_op jit(solution)/shard_map/ppermute | solution.py:39
  191.1 10.7 %psum.37 = bf16[1,256,64]{1,2,0:T(8,128)(2,1)S(1)} all-reduce(f32[1,256,64]{1,2,0:T(8,128)S(1)} %fusion.13), channel_id=1, replica_groups=mesh['gz'=2,'row'=4,'col'=4] {'row'}, use_global_device_ids=true, to_apply=%region_4.5 | all-reduce | flops 16384 | bytes 98304 | tf_op jit(solution)/shard_map/psum | solution.py:65
  201.8 14.4 %all_gather.21 = bf16[1,1024,64]{1,2,0:T(8,128)(2,1)S(1)} all-gather(bf16[1,256,64]{1,2,0:T(8,128)(2,1)S(1)} %psum.37), channel_id=1, replica_groups=mesh['gz'=2,'row'=4,'col'=4] {'col'}, dimensions={1}, use_global_device_ids=true | all-gather | bytes 163840 | tf_op jit(solution)/shard_map/all_gather | solution.py:26
  216.2 1.0 fusion.24
  217.3 3.1 %collective-permute-start.15 = (bf16[2,256,256]{2,1,0:T(8,128)(2,1)S(1)}, bf16[2,256,256]{2,1,0:T(8,128)(2,1)S(1)}, u32[]{:S(2)}, u32[]{:S(2)}) collective-permute-start(bf16[2,256,256]{2,1,0:T(8,128)(2,1)S(1)} %slice.87), channel_id=1, source_target_pairs={{0,3},{1,0},{2,1},{3,2},{4,7},{5,4},{6,5},{7,6},{8,11},{9,8},{10,9... | collective-permute-start | bytes 786440 | tf_op jit(solution)/shard_map/ppermute | solution.py:41
  221.7 1.1 convolution_add_fusion.7
  222.8 7.6 %collective-permute-done.11 = bf16[1,256,256]{2,1,0:T(8,128)(2,1)S(1)} collective-permute-done((bf16[1,256,256]{2,1,0:T(8,128)(2,1)}, bf16[1,256,256]{2,1,0:T(8,128)(2,1)S(1)}, u32[]{:S(2)}, u32[]{:S(2)}) %collective-permute-start.11) | collective-permute-done | bytes 131104 | tf_op jit(solution)/shard_map/ppermute | solution.py:39
  230.7 11.0 %psum.38 = bf16[1,256,64]{1,2,0:T(8,128)(2,1)S(1)} all-reduce(f32[1,256,64]{1,2,0:T(8,128)S(1)} %fusion.4), channel_id=1, replica_groups=mesh['gz'=2,'row'=4,'col'=4] {'row'}, use_global_device_ids=true, to_apply=%region_5.6 | all-reduce | flops 16384 | bytes 98304 | tf_op jit(solution)/shard_map/psum | solution.py:65
  241.6 13.4 %all_gather.22 = bf16[1,1024,64]{1,2,0:T(8,128)(2,1)S(1)} all-gather(bf16[1,256,64]{1,2,0:T(8,128)(2,1)S(1)} %psum.38), channel_id=1, replica_groups=mesh['gz'=2,'row'=4,'col'=4] {'col'}, dimensions={1}, use_global_device_ids=true | all-gather | bytes 163840 | tf_op jit(solution)/shard_map/all_gather | solution.py:26
  255.2 1.1 convolution_add_fusion.5
  256.4 1.1 convolution_add_fusion.3
  258.0 11.5 %all-reduce.7 = bf16[2,256,64]{1,2,0:T(8,128)(2,1)S(1)} all-reduce(f32[2,256,64]{1,2,0:T(8,128)S(1)} %bitcast_subtract_fusion), channel_id=1, replica_groups=mesh['gz'=2,'row'=4,'col'=4] {'row'}, use_global_device_ids=true, to_apply=%region_7.8 | all-reduce | flops 32768 | bytes 196608 | tf_op jit(solution)/shard_map/psum | solution.py:65
  269.5 14.2 %all_gather.23 = bf16[2,1024,64]{1,2,0:T(8,128)(2,1)S(1)} all-gather(bf16[2,256,64]{1,2,0:T(8,128)(2,1)S(1)} %all-reduce.7), channel_id=1, replica_groups=mesh['gz'=2,'row'=4,'col'=4] {'col'}, dimensions={1}, use_global_device_ids=true | all-gather | bytes 327680 | tf_op jit(solution)/shard_map/all_gather | solution.py:26
  (97 shorter events, 13.9 us)
Async XLA Ops:
  7.2 80.8 %all-reduce.4.cloned.1.call-start = ((), (), s32[]{:S(2)}) async-start(), calls=%async_computation | async-start | bytes 131072 | tf_op jit(solution)/shard_map/psum | solution.py:112
  7.2 15.4 %copy-start.5 = (s32[5,2]{0,1:T(2,128)S(1)}, s32[5,2]{0,1:T(2,128)}, u32[]{:S(2)}) copy-start(s32[5,2]{0,1:T(2,128)} %param.18) | copy-start | bytes 124
  7.2 15.5 %copy-start.6 = (s32[2]{0:T(128)S(1)}, s32[2]{0:T(128)}, u32[]{:S(2)}) copy-start(s32[2]{0:T(128)} %param.17) | copy-start | bytes 28
  7.2 16.1 %slice-start.1 = ((bf16[3,256,64]{1,2,0:T(8,128)(2,1)}), bf16[2,256,64]{1,2,0:T(8,128)(2,1)S(1)}, s32[]{:S(2)}) async-start(bf16[3,256,64]{1,2,0:T(8,128)(2,1)} %param.16), calls=%async_computation.3 | async-start | bytes 131072 | tf_op jit(solution)/shard_map/slice | solution.py:110
  8.2 35.0 %copy-start.2 = (bf16[8,256,256]{2,1,0:T(8,128)(2,1)S(1)}, bf16[8,256,256]{2,1,0:T(8,128)(2,1)}, u32[]{:S(2)}) copy-start(bf16[8,256,256]{2,1,0:T(8,128)(2,1)} %param.14) | copy-start | bytes 3145732
  8.3 35.9 %collective-permute-start = (bf16[2,256,256]{2,1,0:T(8,128)(2,1)S(1)}, bf16[2,256,256]{2,1,0:T(8,128)(2,1)S(1)}, u32[]{:S(2)}, u32[]{:S(2)}) collective-permute-start(bf16[2,256,256]{2,1,0:T(8,128)(2,1)S(1)} %slice.68), channel_id=1, source_target_pairs={{0,3},{1,0},{2,1},{3,2},{4,7},{5,4},{6,5},{7,6},{8,11},{9,8},{10,9... | collective-permute-start | bytes 786440 | tf_op jit(solution)/shard_map/ppermute | solution.py:41
  13.4 33.0 %collective-permute-start.1 = (bf16[2,256,256]{2,1,0:T(8,128)(2,1)S(1)}, bf16[2,256,256]{2,1,0:T(8,128)(2,1)S(1)}, u32[]{:S(2)}, u32[]{:S(2)}) collective-permute-start(bf16[2,256,256]{2,1,0:T(8,128)(2,1)S(1)} %slice.68), channel_id=1, source_target_pairs={{0,1},{1,2},{2,3},{3,0},{4,5},{5,6},{6,7},{7,4},{8,9},{9,10},{10,1... | collective-permute-start | bytes 786440 | tf_op jit(solution)/shard_map/ppermute | solution.py:39
  15.0 29.0 %copy-start = (bf16[8,256,256]{2,1,0:T(8,128)(2,1)S(1)}, bf16[8,256,256]{2,1,0:T(8,128)(2,1)}, u32[]{:S(2)}) copy-start(bf16[8,256,256]{2,1,0:T(8,128)(2,1)} %param.13) | copy-start | bytes 3145732
  15.0 87.8 %collective-permute-start.3 = (bf16[1,256,256]{2,1,0:T(8,128)(2,1)}, bf16[1,256,256]{2,1,0:T(8,128)(2,1)}, u32[]{:S(2)}, u32[]{:S(2)}) collective-permute-start(bf16[1,256,256]{2,1,0:T(8,128)(2,1)} %slice.76), channel_id=1, source_target_pairs={{0,3},{1,0},{2,1},{3,2},{4,7},{5,4},{6,5},{7,6},{8,11},{9,8},{10,9... | collective-permute-start | bytes 393224 | tf_op jit(solution)/shard_map/ppermute | solution.py:41
  18.8 84.0 %collective-permute-start.4 = (bf16[1,256,256]{2,1,0:T(8,128)(2,1)}, bf16[1,256,256]{2,1,0:T(8,128)(2,1)}, u32[]{:S(2)}, u32[]{:S(2)}) collective-permute-start(bf16[1,256,256]{2,1,0:T(8,128)(2,1)} %slice.76), channel_id=1, source_target_pairs={{0,1},{1,2},{2,3},{3,0},{4,5},{5,6},{6,7},{7,4},{8,9},{9,10},{10,1... | collective-permute-start | bytes 393224 | tf_op jit(solution)/shard_map/ppermute | solution.py:39
  18.8 162.6 %collective-permute-start.6 = (bf16[1,256,256]{2,1,0:T(8,128)(2,1)}, bf16[1,256,256]{2,1,0:T(8,128)(2,1)}, u32[]{:S(2)}, u32[]{:S(2)}) collective-permute-start(bf16[1,256,256]{2,1,0:T(8,128)(2,1)} %param.11), channel_id=1, source_target_pairs={{0,3},{1,0},{2,1},{3,2},{4,7},{5,4},{6,5},{7,6},{8,11},{9,8},{10,9... | collective-permute-start | bytes 393224 | tf_op jit(solution)/shard_map/ppermute | solution.py:41
  44.1 138.7 %collective-permute-start.7 = (bf16[1,256,256]{2,1,0:T(8,128)(2,1)}, bf16[1,256,256]{2,1,0:T(8,128)(2,1)}, u32[]{:S(2)}, u32[]{:S(2)}) collective-permute-start(bf16[1,256,256]{2,1,0:T(8,128)(2,1)} %param.11), channel_id=1, source_target_pairs={{0,1},{1,2},{2,3},{3,0},{4,5},{5,6},{6,7},{7,4},{8,9},{9,10},{10,1... | collective-permute-start | bytes 393224 | tf_op jit(solution)/shard_map/ppermute | solution.py:39
  46.4 8.7 %collective-permute-start.2 = (bf16[2,256,256]{2,1,0:T(8,128)(2,1)S(1)}, bf16[2,256,256]{2,1,0:T(8,128)(2,1)S(1)}, u32[]{:S(2)}, u32[]{:S(2)}) collective-permute-start(bf16[2,256,256]{2,1,0:T(8,128)(2,1)S(1)} %collective-permute-done.1), channel_id=1, source_target_pairs={{0,1},{1,2},{2,3},{3,0},{4,5},{5,6},{6,7},{7,4},{8,9},{9,10},{10,1... | collective-permute-start | bytes 786440 | tf_op jit(solution)/shard_map/ppermute | solution.py:39
  46.6 9.9 %slice-start = ((bf16[8,256,256]{2,1,0:T(8,128)(2,1)}), bf16[4,256,256]{2,1,0:T(8,128)(2,1)S(1)}, s32[]{:S(2)}) async-start(bf16[8,256,256]{2,1,0:T(8,128)(2,1)} %param.13), calls=%async_computation.2 | async-start | bytes 1048576 | tf_op jit(solution)/shard_map/slice | solution.py:117
  55.1 162.2 %collective-permute-start.9 = (bf16[1,256,256]{2,1,0:T(8,128)(2,1)}, bf16[1,256,256]{2,1,0:T(8,128)(2,1)S(1)}, u32[]{:S(2)}, u32[]{:S(2)}) collective-permute-start(bf16[1,256,256]{2,1,0:T(8,128)(2,1)} %param.12), channel_id=1, source_target_pairs={{0,3},{1,0},{2,1},{3,2},{4,7},{5,4},{6,5},{7,6},{8,11},{9,8},{10,9... | collective-permute-start | bytes 393224 | tf_op jit(solution)/shard_map/ppermute | solution.py:41
  56.3 0.7 copy-start.7
  56.5 46.1 %copy-start.1 = (bf16[8,256,256]{2,1,0:T(8,128)(2,1)S(1)}, bf16[8,256,256]{2,1,0:T(8,128)(2,1)}, u32[]{:S(2)}) copy-start(bf16[8,256,256]{2,1,0:T(8,128)(2,1)} %param.13) | copy-start | bytes 3145732
  57.9 30.1 %slice-start.2 = ((bf16[3,256,64]{1,2,0:T(8,128)(2,1)}), bf16[1,256,64]{1,2,0:T(8,128)(2,1)S(1)}, s32[]{:S(2)}) async-start(bf16[3,256,64]{1,2,0:T(8,128)(2,1)} %param.16), calls=%async_computation.4 | async-start | bytes 65536 | tf_op jit(solution)/shard_map/slice | solution.py:110
  57.9 108.1 %all-reduce.6.cloned.1.call-start = ((), (), s32[]{:S(2)}) async-start(), calls=%async_computation.1 | async-start | bytes 131072 | tf_op jit(solution)/shard_map/psum | solution.py:137
  102.8 117.5 %collective-permute-start.10 = (bf16[1,256,256]{2,1,0:T(8,128)(2,1)}, bf16[1,256,256]{2,1,0:T(8,128)(2,1)}, u32[]{:S(2)}, u32[]{:S(2)}) collective-permute-start(bf16[1,256,256]{2,1,0:T(8,128)(2,1)} %param.12), channel_id=1, source_target_pairs={{0,1},{1,2},{2,3},{3,0},{4,5},{5,6},{6,7},{7,4},{8,9},{9,10},{10,1... | collective-permute-start | bytes 393224 | tf_op jit(solution)/shard_map/ppermute | solution.py:39
  102.8 9.9 %collective-permute-start.5 = (bf16[1,256,256]{2,1,0:T(8,128)(2,1)}, bf16[1,256,256]{2,1,0:T(8,128)(2,1)S(1)}, u32[]{:S(2)}, u32[]{:S(2)}) collective-permute-start(bf16[1,256,256]{2,1,0:T(8,128)(2,1)} %collective-permute-done.4), channel_id=1, source_target_pairs={{0,1},{1,2},{2,3},{3,0},{4,5},{5,6},{6,7},{7,4},{8,9},{9,10},{10,1... | collective-permute-start | bytes 393224 | tf_op jit(solution)/shard_map/ppermute | solution.py:39
  103.9 8.8 %copy-start.3 = (bf16[1,256,256]{2,1,0:T(8,128)(2,1)S(1)}, bf16[1,256,256]{2,1,0:T(8,128)(2,1)}, u32[]{:S(2)}) copy-start(bf16[1,256,256]{2,1,0:T(8,128)(2,1)} %slice.82) | copy-start | bytes 393220
  112.7 142.5 %collective-permute-start.12 = (bf16[1,256,256]{2,1,0:T(8,128)(2,1)S(1)}, bf16[1,256,256]{2,1,0:T(8,128)(2,1)}, u32[]{:S(2)}, u32[]{:S(2)}) collective-permute-start(bf16[1,256,256]{2,1,0:T(8,128)(2,1)S(1)} %copy-done.3), channel_id=1, source_target_pairs={{0,3},{1,0},{2,1},{3,2},{4,7},{5,4},{6,5},{7,6},{8,11},{9,8},{10,9... | collective-permute-start | bytes 393224 | tf_op jit(solution)/shard_map/ppermute | solution.py:41
  113.9 52.1 %copy-start.4 = (bf16[1,256,64]{1,2,0:T(8,128)(2,1)S(1)}, bf16[1,256,64]{1,2,0:T(8,128)(2,1)}, u32[]{:S(2)}) copy-start(bf16[1,256,64]{1,2,0:T(8,128)(2,1)} %param.15) | copy-start | bytes 98308
  181.3 39.0 %collective-permute-start.13 = (bf16[1,256,256]{2,1,0:T(8,128)(2,1)S(1)}, bf16[1,256,256]{2,1,0:T(8,128)(2,1)S(1)}, u32[]{:S(2)}, u32[]{:S(2)}) collective-permute-start(bf16[1,256,256]{2,1,0:T(8,128)(2,1)S(1)} %copy-done.3), channel_id=1, source_target_pairs={{0,1},{1,2},{2,3},{3,0},{4,5},{5,6},{6,7},{7,4},{8,9},{9,10},{10,1... | collective-permute-start | bytes 393224 | tf_op jit(solution)/shard_map/ppermute | solution.py:39
  182.9 7.8 %collective-permute-start.8 = (bf16[1,256,256]{2,1,0:T(8,128)(2,1)}, bf16[1,256,256]{2,1,0:T(8,128)(2,1)S(1)}, u32[]{:S(2)}, u32[]{:S(2)}) collective-permute-start(bf16[1,256,256]{2,1,0:T(8,128)(2,1)} %collective-permute-done.7), channel_id=1, source_target_pairs={{0,1},{1,2},{2,3},{3,0},{4,5},{5,6},{6,7},{7,4},{8,9},{9,10},{10,1... | collective-permute-start | bytes 393224 | tf_op jit(solution)/shard_map/ppermute | solution.py:39
  190.7 29.9 %collective-permute-start.16 = (bf16[2,256,256]{2,1,0:T(8,128)(2,1)S(1)}, bf16[2,256,256]{2,1,0:T(8,128)(2,1)S(1)}, u32[]{:S(2)}, u32[]{:S(2)}) collective-permute-start(bf16[2,256,256]{2,1,0:T(8,128)(2,1)S(1)} %slice.87), channel_id=1, source_target_pairs={{0,1},{1,2},{2,3},{3,0},{4,5},{5,6},{6,7},{7,4},{8,9},{9,10},{10,1... | collective-permute-start | bytes 786440 | tf_op jit(solution)/shard_map/ppermute | solution.py:39
  217.3 66.9 %collective-permute-start.15 = (bf16[2,256,256]{2,1,0:T(8,128)(2,1)S(1)}, bf16[2,256,256]{2,1,0:T(8,128)(2,1)S(1)}, u32[]{:S(2)}, u32[]{:S(2)}) collective-permute-start(bf16[2,256,256]{2,1,0:T(8,128)(2,1)S(1)} %slice.87), channel_id=1, source_target_pairs={{0,3},{1,0},{2,1},{3,2},{4,7},{5,4},{6,5},{7,6},{8,11},{9,8},{10,9... | collective-permute-start | bytes 786440 | tf_op jit(solution)/shard_map/ppermute | solution.py:41
  220.3 10.0 %collective-permute-start.11 = (bf16[1,256,256]{2,1,0:T(8,128)(2,1)}, bf16[1,256,256]{2,1,0:T(8,128)(2,1)S(1)}, u32[]{:S(2)}, u32[]{:S(2)}) collective-permute-start(bf16[1,256,256]{2,1,0:T(8,128)(2,1)} %collective-permute-done.10), channel_id=1, source_target_pairs={{0,1},{1,2},{2,3},{3,0},{4,5},{5,6},{6,7},{7,4},{8,9},{9,10},{10,1... | collective-permute-start | bytes 393224 | tf_op jit(solution)/shard_map/ppermute | solution.py:39
  220.3 36.0 %collective-permute-start.14 = (bf16[1,256,256]{2,1,0:T(8,128)(2,1)S(1)}, bf16[1,256,256]{2,1,0:T(8,128)(2,1)}, u32[]{:S(2)}, u32[]{:S(2)}) collective-permute-start(bf16[1,256,256]{2,1,0:T(8,128)(2,1)S(1)} %collective-permute-done.13), channel_id=1, source_target_pairs={{0,1},{1,2},{2,3},{3,0},{4,5},{5,6},{6,7},{7,4},{8,9},{9,10},{10,1... | collective-permute-start | bytes 393224 | tf_op jit(solution)/shard_map/ppermute | solution.py:39
  220.5 63.8 %collective-permute-start.17 = (bf16[2,256,256]{2,1,0:T(8,128)(2,1)S(1)}, bf16[2,256,256]{2,1,0:T(8,128)(2,1)S(1)}, u32[]{:S(2)}, u32[]{:S(2)}) collective-permute-start(bf16[2,256,256]{2,1,0:T(8,128)(2,1)S(1)} %collective-permute-done.16), channel_id=1, source_target_pairs={{0,1},{1,2},{2,3},{3,0},{4,5},{5,6},{6,7},{7,4},{8,9},{9,10},{10,1... | collective-permute-start | bytes 786440 | tf_op jit(solution)/shard_map/ppermute | solution.py:39
Sparse Core Ops, SparseCore 0:
  58.0 29.9 all-reduce.3
  113.9 52.1 all-reduce.5
